TPU v7x, 512 devices: a whole 4x8x8 slice. The times are simulated.
512 devices in a mesh: tm: 4 (over y_hi, core), pix: 128 (over x, z, y_lo).
Axes of the slice: x: 4, y: 8 (y_hi: 2, y_lo: 4; y = y_hi * 4 + y_lo), z: 8, core: 2. Of those that a mesh axis runs over, the one named last changes fastest.
Arguments:
- activations: bfloat16 [4, 327680, 256], P('tm', 'pix'), may hold values from -6 to 6
- down_weight: bfloat16 [1024, 256], replicated, may hold values from -0.1875 to 0.1875
- down_bias: float32 [256], replicated, may hold values from -3 to 3
- taps: float32 [9, 256], replicated, may hold values from -2 to 2
- point_weight: bfloat16 [256, 256], replicated, may hold values from -0.375 to 0.375
- time_mix: float32 [4, 4, 256], replicated, may hold values from -3 to 3
- edge_rows: int32 [128, 2, 20], P('pix'), may hold values from 0 to 19, as said below
- cotangent: bfloat16 [4, 81920, 256], P(None, ('pix', 'tm')), may hold values from -6 to 6
Outputs:
- grad_input: bfloat16 [4, 327680, 256], P('tm', 'pix')
- grad_down: float32 [1024, 256], replicated
- grad_bias: float32 [256], replicated
- grad_taps: float32 [9, 256], replicated
- grad_point: float32 [256, 256], replicated
- grad_mix: float32 [4, 4, 256], replicated
Inputs may be any that keep to these rules, and one draw needn't show every extreme that they name: Each edge_rows[t, e] is either 0, 1, .., 19 or its reversal; edge_rows[t, 1] equals edge_rows[(t + 1) mod 128, 0].
All inputs are finite; a program needn't handle non-finite values.
Results may differ from a plain program's by a relative error of at most 0.014.
Values may be sent and summed in bfloat16 or wider, within the bound.
No kernel may reach another device: no remote copies, remote signals or barrier semaphores. Data moves between devices by JAX's collectives and lax.ppermute only.
A program may use at most 64 MiB of HBM per device.

v0:
```python
import math
import jax
import jax.numpy as jnp
from jax import lax
from jax.sharding import Mesh, PartitionSpec as P

C = 256
TR = 20
TC = 32
TM = ("yh", "core")
PIX = ("x", "z", "yl")
RING = ("yh", "yl")
SUM_ROWS = 1306
PAD_ROWS = 1536


def padded_2(cells, sides, width):
    for axis, dim in sides:
        count = lax.axis_size(axis)
        head = lax.slice_in_dim(cells, 0, width, axis=dim)
        tail = lax.slice_in_dim(cells, cells.shape[dim] - width, cells.shape[dim], axis=dim)
        cells = jnp.concatenate(
            [
                lax.ppermute(tail, axis, [(i, (i + 1) % count) for i in range(count)]),
                cells,
                lax.ppermute(head, axis, [((i + 1) % count, i) for i in range(count)]),
            ],
            axis=dim,
        )
    return cells


def scatter_sum(rows, axis):
    count = lax.axis_size(axis)
    low = rows.astype(jnp.bfloat16).reshape(count, rows.shape[0] // count, C)
    got = lax.all_to_all(low, axis, split_axis=0, concat_axis=0, tiled=True)
    return jnp.sum(got.astype(jnp.float32), axis=0)


def copies(rows, axis):
    count = lax.axis_size(axis)
    wide = jnp.broadcast_to(rows[None], (count,) + rows.shape)
    return lax.all_to_all(wide, axis, split_axis=0, concat_axis=0, tiled=True)


def sum_over_devices(parts):
    half = PAD_ROWS // 2
    core = lax.axis_index("core")
    keep = lax.dynamic_slice_in_dim(parts, core * half, half, axis=0)
    send = lax.dynamic_slice_in_dim(parts, (1 - core) * half, half, axis=0)
    got = lax.ppermute(send.astype(jnp.bfloat16), "core", [(0, 1), (1, 0)])
    rows = keep + got.astype(jnp.float32)
    rows = scatter_sum(rows, "x")
    rows = scatter_sum(rows, "z")
    rows = jnp.sum(copies(rows.astype(jnp.bfloat16), RING).astype(jnp.float32), axis=0)
    rows = rows.astype(jnp.bfloat16)
    rows = copies(rows, "z").reshape(-1, C)
    rows = copies(rows, "x").reshape(-1, C)
    rows = lax.all_gather(rows, "core", axis=0, tiled=True)
    return rows.astype(jnp.float32)


def on_device(
    activations, down_weight, down_bias, taps, point_weight, time_mix, edge_rows, cotangent
):
    frames = lax.axis_size(TM)
    tiles = lax.axis_size(PIX)
    pixels = TR * TC
    scale = 1.0 / math.sqrt(frames * tiles * pixels)
    rows_in = activations.reshape(pixels, 4 * C)
    preact = jnp.dot(rows_in, down_weight, preferred_element_type=jnp.float32) + down_bias
    pooled = jax.nn.silu(preact).astype(jnp.bfloat16)
    tile_grid = pooled.reshape(1, TR, TC, C)
    padded = padded_2(tile_grid, ((PIX, 2),), 1)
    west_map = edge_rows[0, 0]
    east_map = edge_rows[0, 1]
    west_col = jnp.take(padded[0, :, 0, :], west_map, axis=0)
    east_col = jnp.take(padded[0, :, TC + 1, :], east_map, axis=0)
    widened = jnp.concatenate([west_col[:, None, :], tile_grid[0], east_col[:, None, :]], axis=1)
    widened = jnp.pad(widened, ((1, 1), (0, 0), (0, 0)))
    spread = jnp.zeros((TR, TC, C), jnp.float32)
    for row_off in range(3):
        for col_off in range(3):
            spread = (
                spread
                + taps[row_off * 3 + col_off]
                * widened[row_off : row_off + TR, col_off : col_off + TC, :]
            )
    spread_low = spread.astype(jnp.bfloat16).reshape(pixels, C)
    mixed_in = (
        pooled.astype(jnp.float32)
        + jnp.dot(spread_low, point_weight, preferred_element_type=jnp.float32)
    ).astype(jnp.bfloat16)
    by_pixel = lax.all_to_all(
        mixed_in.reshape(1, pixels, C), TM, split_axis=1, concat_axis=0, tiled=True
    )
    mix_part = jnp.einsum("gpc,fpc->fgc", by_pixel, cotangent, preferred_element_type=jnp.float32)
    cot_f = cotangent.astype(jnp.float32)
    mixed_acc = jnp.zeros((frames, cotangent.shape[1], C), jnp.float32)
    for source in range(frames):
        mixed_acc = mixed_acc + time_mix[source][:, None, :] * cot_f[source][None, :, :]
    mixed_grad = mixed_acc.astype(jnp.bfloat16)
    back_grad = lax.all_to_all(mixed_grad, TM, split_axis=0, concat_axis=1, tiled=True)
    mixed_rows = back_grad.reshape(pixels, C)
    point_part = jnp.dot(spread_low.T, mixed_rows, preferred_element_type=jnp.float32)
    spread_grad = jnp.dot(mixed_rows, point_weight.T, preferred_element_type=jnp.float32).astype(
        jnp.bfloat16
    )
    grad_float = spread_grad.reshape(TR, TC, C).astype(jnp.float32)
    taps_rows = []
    for row_off in range(3):
        for col_off in range(3):
            taps_rows.append(
                jnp.sum(
                    grad_float * widened[row_off : row_off + TR, col_off : col_off + TC, :],
                    axis=(0, 1),
                )
            )
    taps_part = jnp.stack(taps_rows, axis=0)
    grad_padded = jnp.pad(grad_float, ((2, 2), (2, 2), (0, 0)))
    wide_grad = jnp.zeros((TR + 2, TC + 2, C), jnp.float32)
    for row_off in range(3):
        for col_off in range(3):
            wide_grad = (
                wide_grad
                + taps[row_off * 3 + col_off]
                * grad_padded[2 - row_off : 4 - row_off + TR, 2 - col_off : 4 - col_off + TC, :]
            )
    west_back = jnp.take(wide_grad[1 : TR + 1, 0, :], west_map, axis=0)
    east_back = jnp.take(wide_grad[1 : TR + 1, TC + 1, :], east_map, axis=0)
    outgoing = jnp.stack([west_back, east_back], axis=1)
    incoming = padded_2(outgoing.astype(jnp.bfloat16), ((PIX, 1),), 1).astype(outgoing.dtype)
    inner_grad = wide_grad[1 : TR + 1, 1 : TC + 1, :]
    inner_grad = inner_grad.at[:, 0, :].add(incoming[:, 0, :])
    inner_grad = inner_grad.at[:, TC - 1, :].add(incoming[:, 3, :])
    pooled_grad = mixed_rows.astype(jnp.float32) + inner_grad.reshape(pixels, C)
    sigma = jax.nn.sigmoid(preact)
    pre_grad = (pooled_grad * (sigma * (1.0 + preact * (1.0 - sigma)))).astype(jnp.bfloat16)
    bias_part = jnp.sum(pre_grad.astype(jnp.float32), axis=0)
    down_part = jnp.dot(rows_in.T, pre_grad, preferred_element_type=jnp.float32)
    grad_input = jnp.dot(pre_grad, down_weight.T, preferred_element_type=jnp.float32).astype(
        jnp.bfloat16
    )
    parts = jnp.concatenate(
        [
            down_part,
            point_part,
            mix_part.reshape(frames * frames, C),
            taps_part,
            bias_part.reshape(1, C),
            jnp.zeros((PAD_ROWS - SUM_ROWS, C), jnp.float32),
        ],
        axis=0,
    )
    total = sum_over_devices(parts) * scale
    grad_down = total[:1024]
    grad_point = total[1024:1280]
    grad_mix = total[1280:1296].reshape(frames, frames, C)
    grad_taps = total[1296:1305]
    grad_bias = total[1305]
    return (
        grad_input.reshape(1, 4 * pixels, C),
        grad_down,
        grad_bias,
        grad_taps,
        grad_point,
        grad_mix,
    )


def solution(mesh):
    chips = Mesh(mesh.devices.reshape(2, 2, 4, 8, 4), ("yh", "core", "x", "z", "yl"))
    in_specs = (
        P(TM, PIX, None),
        P(),
        P(),
        P(),
        P(),
        P(),
        P(PIX, None, None),
        P(None, PIX + TM, None),
    )
    out_specs = (P(TM, PIX, None), P(), P(), P(), P(), P())
    return jax.shard_map(
        on_device, mesh=chips, in_specs=in_specs, out_specs=out_specs, check_vma=False
    )
```

profile of v0, /device:TPU:1, one launch (start us, length us, event | category | flops | bytes accessed | tf_op | source)
XLA Modules:
  0.0 167.9 jit_solution(9329589787763400051)
XLA Ops:
  1.4 1.0 convert_element_type.105
  3.5 10.3 %all-to-all-start = ((bf16[4,160,256]{2,1,0:T(8,128)(2,1)}), bf16[4,160,256]{2,1,0:T(8,128)(2,1)S(1)}, u32[]{:S(2)}, u32[]{:S(2)}) async-start(bf16[4,160,256]{2,1,0:T(8,128)(2,1)} %add_convert_fusion.1), calls=%async_computation | async-start | bytes 655360 | tf_op jit(solution)/shard_map/all_to_all | solution.py:103
  13.8 9.8 %all-to-all-done = bf16[4,160,256]{2,1,0:T(8,128)(2,1)S(1)} async-done(((bf16[4,160,256]{2,1,0:T(8,128)(2,1)}), bf16[4,160,256]{2,1,0:T(8,128)(2,1)S(1)}, u32[]{:S(2)}, u32[]{:S(2)}) %all-to-all-start) | async-done | bytes 327712 | tf_op jit(solution)/shard_map/all_to_all | solution.py:103
  26.5 11.3 %collective-permute-start.1 = (bf16[20,1,256]{2,0,1:T(8,128)(2,1)S(1)}, bf16[20,1,256]{2,0,1:T(8,128)(2,1)S(1)}, u32[]{:S(2)}, u32[]{:S(2)}) collective-permute-start(bf16[20,1,256]{2,0,1:T(8,128)(2,1)S(1)} %fusion.49), channel_id=1, source_target_pairs={{1,0},{2,1},{3,2},{4,3},{5,4},{6,5},{7,6},{8,7},{9,8},{10,9},{11,1... | collective-permute-start | bytes 30728 | tf_op jit(solution)/shard_map/ppermute | solution.py:26
  38.5 1.9 %collective-permute-start = (bf16[20,1,256]{2,0,1:T(8,128)(2,1)S(1)}, bf16[20,1,256]{2,0,1:T(8,128)(2,1)S(1)}, u32[]{:S(2)}, u32[]{:S(2)}) collective-permute-start(bf16[20,1,256]{2,0,1:T(8,128)(2,1)S(1)} %fusion.48), channel_id=1, source_target_pairs={{0,1},{1,2},{2,3},{3,4},{4,5},{5,6},{6,7},{7,8},{8,9},{9,10},{10,1... | collective-permute-start | bytes 30728 | tf_op jit(solution)/shard_map/ppermute | solution.py:24
  40.5 1.0 copy.110
  41.5 2.5 %reshape.148 = bf16[640,1024]{1,0:T(8,128)(2,1)S(1)} reshape(bf16[1,2560,256]{2,1,0:T(8,128)(2,1)} %param.16) | data formatting | bytes 2621440 | tf_op jit(solution)/shard_map/reshape | solution.py:70
  44.0 1.2 slice.277
  45.3 3.7 %collective-permute-done = bf16[20,1,256]{2,0,1:T(8,128)(2,1)S(1)} collective-permute-done((bf16[20,1,256]{2,0,1:T(8,128)(2,1)S(1)}, bf16[20,1,256]{2,0,1:T(8,128)(2,1)S(1)}, u32[]{:S(2)}, u32[]{:S(2)}) %collective-permute-start) | collective-permute-done | bytes 10272 | tf_op jit(solution)/shard_map/ppermute | solution.py:24
  50.8 5.7 %collective-permute-start.3 = (bf16[1,20,1,256]{3,1,2,0:T(8,128)(2,1)S(1)}, bf16[1,20,1,256]{3,1,2,0:T(8,128)(2,1)S(1)}, u32[]{:S(2)}, u32[]{:S(2)}) collective-permute-start(bf16[1,20,1,256]{3,1,2,0:T(8,128)(2,1)S(1)} %copy.128), channel_id=1, source_target_pairs={{1,0},{2,1},{3,2},{4,3},{5,4},{6,5},{7,6},{8,7},{9,8},{10,9},{11,1... | collective-permute-start | bytes 30728 | tf_op jit(solution)/shard_map/ppermute | solution.py:26
  56.5 1.9 %collective-permute-start.2 = (bf16[1,20,1,256]{3,1,2,0:T(8,128)(2,1)S(1)}, bf16[1,20,1,256]{3,1,2,0:T(8,128)(2,1)S(1)}, u32[]{:S(2)}, u32[]{:S(2)}) collective-permute-start(bf16[1,20,1,256]{3,1,2,0:T(8,128)(2,1)S(1)} %copy.127), channel_id=1, source_target_pairs={{0,1},{1,2},{2,3},{3,4},{4,5},{5,6},{6,7},{7,8},{8,9},{9,10},{10,1... | collective-permute-start | bytes 30728 | tf_op jit(solution)/shard_map/ppermute | solution.py:24
  58.4 1.6 convolution_bitcast_fusion
  62.2 4.8 %collective-permute-done.2 = bf16[1,20,1,256]{3,1,2,0:T(8,128)(2,1)S(1)} collective-permute-done((bf16[1,20,1,256]{3,1,2,0:T(8,128)(2,1)S(1)}, bf16[1,20,1,256]{3,1,2,0:T(8,128)(2,1)S(1)}, u32[]{:S(2)}, u32[]{:S(2)}) %collective-permute-start.2) | collective-permute-done | bytes 10272 | tf_op jit(solution)/shard_map/ppermute | solution.py:24
  70.0 3.4 %reduce.8 = bf16[640,256]{1,0:T(8,128)(2,1)} reduce(bf16[640,1,256]{2,1,0:T(2,128)(2,1)S(1)} %bitcast.109, bf16[]{:T(256)} %broadcast.133), dimensions={1}, to_apply=%bitcast.98.reduce_sub_computation | reduce | bytes 655362
  73.4 1.8 %reshape.204 = bf16[4,2,20480]{2,1,0:T(2,128)(2,1)} reshape(bf16[640,256]{1,0:T(8,128)(2,1)} %reduce.8) | data formatting | bytes 655360
  75.1 6.4 %all-to-all-start.1 = ((bf16[4,2,20480]{2,1,0:T(2,128)(2,1)}), bf16[4,2,20480]{2,1,0:T(2,128)(2,1)S(1)}, u32[]{:S(2)}, u32[]{:S(2)}) async-start(bf16[4,2,20480]{2,1,0:T(2,128)(2,1)} %reshape.204), calls=%async_computation.1 | async-start | bytes 655360 | tf_op jit(solution)/shard_map/all_to_all | solution.py:94
  88.6 1.0 fusion.53
  89.6 1.7 %all-to-all-done.1 = bf16[4,2,20480]{2,1,0:T(2,128)(2,1)S(1)} async-done(((bf16[4,2,20480]{2,1,0:T(2,128)(2,1)}), bf16[4,2,20480]{2,1,0:T(2,128)(2,1)S(1)}, u32[]{:S(2)}, u32[]{:S(2)}) %all-to-all-start.1) | async-done | bytes 327712 | tf_op jit(solution)/shard_map/all_to_all | solution.py:94
  91.7 1.1 copy.109
  92.8 1.5 convolution_bitcast_fusion.1
  96.0 3.0 %concatenate.24 = f32[1536,256]{0,1:T(8,128)S(1)} concatenate(f32[1024,256]{0,1:T(8,128)S(1)} %copy-done.1, f32[256,256]{0,1:T(8,128)S(1)} %copy-done.6, f32[16,256]{0,1:T(8,128)} %copy.113, f32[1,256]{0,1:T(8,128)} %copy.114, f32[1,256]{0,1:T(8,128)} %copy.115, f32[1,256]{0,1:T(8,128)} %copy.116, f32[1,256]{0,1:T(8,128)} %copy.117, f32[1,256]{0,1:T(8,128)} %copy.118, ...), dimensions={0} | concatenate | bytes 3145728 | tf_op jit(solution)/shard_map/concatenate | solution.py:144
  99.1 2.8 %collective-permute-start.4 = (bf16[768,256]{0,1:T(8,128)(2,1)S(1)}, bf16[768,256]{0,1:T(8,128)(2,1)S(1)}, u32[]{:S(2)}, u32[]{:S(2)}) collective-permute-start(bf16[768,256]{0,1:T(8,128)(2,1)S(1)} %dynamic-slice_convert_fusion), channel_id=1, source_target_pairs={{0,128},{128,0},{1,129},{129,1},{2,130},{130,2},{3,131},{131,3},{4... | collective-permute-start | bytes 1179656 | tf_op jit(solution)/shard_map/ppermute | solution.py:51
  101.9 1.3 collective-permute-done.4
  103.5 10.2 %all_to_all.46 = bf16[4,192,256]{2,1,0:T(8,128)(2,1)S(1)} all-to-all(bf16[4,192,256]{2,1,0:T(8,128)(2,1)S(1)} %bitcast.111), channel_id=1, replica_groups=mesh['yh'=2,'core'=2,'x'=4,'z'=8,'yl'=4] {'x'}, dimensions={0} | all-to-all | bytes 786432 | tf_op jit(solution)/shard_map/all_to_all | solution.py:36
  113.8 10.2 %all_to_all.47 = bf16[8,24,256]{2,1,0:T(8,128)(2,1)S(1)} all-to-all(bf16[8,24,256]{2,1,0:T(8,128)(2,1)S(1)} %bitcast.116), channel_id=1, replica_groups=mesh['yh'=2,'core'=2,'x'=4,'z'=8,'yl'=4] {'z'}, dimensions={0} | all-to-all | bytes 196608 | tf_op jit(solution)/shard_map/all_to_all | solution.py:36
  124.0 11.8 %all_to_all.48 = bf16[8,24,256]{2,1,0:T(8,128)(2,1)S(1)} all-to-all(bf16[8,24,256]{2,1,0:T(8,128)(2,1)S(1)} %broadcast_in_dim.50), channel_id=1, replica_groups=mesh['yh'=2,'core'=2,'x'=4,'z'=8,'yl'=4] {'yh','yl'}, dimensions={0} | all-to-all | bytes 196608 | tf_op jit(solution)/shard_map/all_to_all | solution.py:43
  135.8 10.0 %all_to_all.49 = bf16[8,24,256]{2,1,0:T(8,128)(2,1)S(1)} all-to-all(bf16[8,24,256]{2,1,0:T(8,128)(2,1)S(1)} %broadcast_in_dim.51), channel_id=1, replica_groups=mesh['yh'=2,'core'=2,'x'=4,'z'=8,'yl'=4] {'z'}, dimensions={0} | all-to-all | bytes 196608 | tf_op jit(solution)/shard_map/all_to_all | solution.py:43
  146.6 3.5 %all-to-all-start.6 = ((bf16[4,192,256]{2,1,0:T(8,128)(2,1)}), bf16[4,192,256]{2,1,0:T(8,128)(2,1)S(1)}, u32[]{:S(2)}, u32[]{:S(2)}) async-start(bf16[4,192,256]{2,1,0:T(8,128)(2,1)} %broadcast_in_dim.53), calls=%async_computation.6 | async-start | bytes 786432 | tf_op jit(solution)/shard_map/all_to_all | solution.py:43
  150.6 1.6 reshape.149
  152.2 4.0 %all-to-all-done.6 = bf16[4,192,256]{2,1,0:T(8,128)(2,1)S(1)} async-done(((bf16[4,192,256]{2,1,0:T(8,128)(2,1)}), bf16[4,192,256]{2,1,0:T(8,128)(2,1)S(1)}, u32[]{:S(2)}, u32[]{:S(2)}) %all-to-all-start.6) | async-done | bytes 393248 | tf_op jit(solution)/shard_map/all_to_all | solution.py:43
  156.2 8.0 %all_gather.3 = bf16[1536,256]{1,0:T(8,128)(2,1)S(1)} all-gather(bf16[768,256]{1,0:T(8,128)(2,1)S(1)} %bitcast.112), channel_id=1, replica_groups=mesh['yh'=2,'core'=2,'x'=4,'z'=8,'yl'=4] {'core'}, dimensions={0}, use_global_device_ids=true | all-gather | bytes 1179648 | tf_op jit(solution)/shard_map/all_gather | solution.py:59
  166.2 1.0 slice.290
  (91 shorter events, 25.8 us)
Async XLA Ops:
  0.6 49.3 %copy-start = (bf16[1024,256]{1,0:T(8,128)(2,1)S(1)}, bf16[1024,256]{1,0:T(8,128)(2,1)}, u32[]{:S(2)}) copy-start(bf16[1024,256]{1,0:T(8,128)(2,1)} %param.17) | copy-start | bytes 1572868
  2.5 11.3 %copy-start.10 = (s32[1,2,20]{2,1,0:T(2,128)S(1)}, s32[1,2,20]{2,1,0:T(2,128)}, u32[]{:S(2)}) copy-start(s32[1,2,20]{2,1,0:T(2,128)} %param.22) | copy-start | bytes 484
  2.5 11.3 %copy-start.9 = (f32[9,256]{1,0:T(8,128)S(1)}, f32[9,256]{1,0:T(8,128)}, u32[]{:S(2)}) copy-start(f32[9,256]{1,0:T(8,128)} %param.19) | copy-start | bytes 27652
  2.5 21.2 %copy-start.7 = (bf16[256,256]{1,0:T(8,128)(2,1)S(1)}, bf16[256,256]{1,0:T(8,128)(2,1)}, u32[]{:S(2)}) copy-start(bf16[256,256]{1,0:T(8,128)(2,1)} %param.20) | copy-start | bytes 393220
  3.5 20.2 %all-to-all-start = ((bf16[4,160,256]{2,1,0:T(8,128)(2,1)}), bf16[4,160,256]{2,1,0:T(8,128)(2,1)S(1)}, u32[]{:S(2)}, u32[]{:S(2)}) async-start(bf16[4,160,256]{2,1,0:T(8,128)(2,1)} %add_convert_fusion.1), calls=%async_computation | async-start | bytes 655360 | tf_op jit(solution)/shard_map/all_to_all | solution.py:103
  24.3 16.1 %copy-start.3 = (bf16[4,160,256]{2,1,0:T(8,128)(2,1)S(1)}, bf16[4,160,256]{2,1,0:T(8,128)(2,1)}, u32[]{:S(2)}) copy-start(bf16[4,160,256]{2,1,0:T(8,128)(2,1)} %param.23) | copy-start | bytes 983044
  24.9 0.9 copy-start.2
  26.5 18.7 %collective-permute-start.1 = (bf16[20,1,256]{2,0,1:T(8,128)(2,1)S(1)}, bf16[20,1,256]{2,0,1:T(8,128)(2,1)S(1)}, u32[]{:S(2)}, u32[]{:S(2)}) collective-permute-start(bf16[20,1,256]{2,0,1:T(8,128)(2,1)S(1)} %fusion.49), channel_id=1, source_target_pairs={{1,0},{2,1},{3,2},{4,3},{5,4},{6,5},{7,6},{8,7},{9,8},{10,9},{11,1... | collective-permute-start | bytes 30728 | tf_op jit(solution)/shard_map/ppermute | solution.py:26
  38.5 10.4 %collective-permute-start = (bf16[20,1,256]{2,0,1:T(8,128)(2,1)S(1)}, bf16[20,1,256]{2,0,1:T(8,128)(2,1)S(1)}, u32[]{:S(2)}, u32[]{:S(2)}) collective-permute-start(bf16[20,1,256]{2,0,1:T(8,128)(2,1)S(1)} %fusion.48), channel_id=1, source_target_pairs={{0,1},{1,2},{2,3},{3,4},{4,5},{5,6},{6,7},{7,8},{8,9},{9,10},{10,1... | collective-permute-start | bytes 30728 | tf_op jit(solution)/shard_map/ppermute | solution.py:24
  44.0 5.9 %copy-start.11 = (f32[256]{0:T(256)S(1)}, f32[256]{0:T(256)}, u32[]{:S(2)}) copy-start(f32[256]{0:T(256)} %param.18) | copy-start | bytes 3076
  50.8 9.3 %copy-start.4 = (bf16[640,256]{1,0:T(8,128)(2,1)}, bf16[640,256]{1,0:T(8,128)(2,1)S(1)}, u32[]{:S(2)}) copy-start(bf16[640,256]{1,0:T(8,128)(2,1)S(1)} %get-tuple-element.53) | copy-start | bytes 983044
  50.8 10.8 %collective-permute-start.3 = (bf16[1,20,1,256]{3,1,2,0:T(8,128)(2,1)S(1)}, bf16[1,20,1,256]{3,1,2,0:T(8,128)(2,1)S(1)}, u32[]{:S(2)}, u32[]{:S(2)}) collective-permute-start(bf16[1,20,1,256]{3,1,2,0:T(8,128)(2,1)S(1)} %copy.128), channel_id=1, source_target_pairs={{1,0},{2,1},{3,2},{4,3},{5,4},{6,5},{7,6},{8,7},{9,8},{10,9},{11,1... | collective-permute-start | bytes 30728 | tf_op jit(solution)/shard_map/ppermute | solution.py:26
  56.5 10.5 %collective-permute-start.2 = (bf16[1,20,1,256]{3,1,2,0:T(8,128)(2,1)S(1)}, bf16[1,20,1,256]{3,1,2,0:T(8,128)(2,1)S(1)}, u32[]{:S(2)}, u32[]{:S(2)}) collective-permute-start(bf16[1,20,1,256]{3,1,2,0:T(8,128)(2,1)S(1)} %copy.127), channel_id=1, source_target_pairs={{0,1},{1,2},{2,3},{3,4},{4,5},{5,6},{6,7},{7,8},{8,9},{9,10},{10,1... | collective-permute-start | bytes 30728 | tf_op jit(solution)/shard_map/ppermute | solution.py:24
  75.1 16.2 %all-to-all-start.1 = ((bf16[4,2,20480]{2,1,0:T(2,128)(2,1)}), bf16[4,2,20480]{2,1,0:T(2,128)(2,1)S(1)}, u32[]{:S(2)}, u32[]{:S(2)}) async-start(bf16[4,2,20480]{2,1,0:T(2,128)(2,1)} %reshape.204), calls=%async_computation.1 | async-start | bytes 655360 | tf_op jit(solution)/shard_map/all_to_all | solution.py:94
  89.6 3.1 %copy-start.8 = (bf16[4,160,256]{1,0,2:T(4,128)(2,1)S(1)}, bf16[4,160,256]{1,0,2:T(4,128)(2,1)}, u32[]{:S(2)}) copy-start(bf16[4,160,256]{1,0,2:T(4,128)(2,1)} %copy.110) | copy-start | bytes 983044
  92.8 3.3 %copy-start.1 = (f32[1024,256]{0,1:T(8,128)S(1)}, f32[1024,256]{0,1:T(8,128)}, u32[]{:S(2)}) copy-start(f32[1024,256]{0,1:T(8,128)} %convolution_bitcast_fusion) | copy-start | bytes 3145732
  92.8 3.3 %copy-start.6 = (f32[256,256]{0,1:T(8,128)S(1)}, f32[256,256]{0,1:T(8,128)}, u32[]{:S(2)}) copy-start(f32[256,256]{0,1:T(8,128)} %fusion.53) | copy-start | bytes 786436
  99.1 4.1 %collective-permute-start.4 = (bf16[768,256]{0,1:T(8,128)(2,1)S(1)}, bf16[768,256]{0,1:T(8,128)(2,1)S(1)}, u32[]{:S(2)}, u32[]{:S(2)}) collective-permute-start(bf16[768,256]{0,1:T(8,128)(2,1)S(1)} %dynamic-slice_convert_fusion), channel_id=1, source_target_pairs={{0,128},{128,0},{1,129},{129,1},{2,130},{130,2},{3,131},{131,3},{4... | collective-permute-start | bytes 1179656 | tf_op jit(solution)/shard_map/ppermute | solution.py:51
  113.7 36.3 %copy-start.5 = (bf16[640,256]{1,0:T(8,128)(2,1)S(1)}, bf16[640,256]{1,0:T(8,128)(2,1)}, u32[]{:S(2)}) copy-start(bf16[640,256]{1,0:T(8,128)(2,1)} %copy-done.4) | copy-start | bytes 983044
  146.6 9.7 %all-to-all-start.6 = ((bf16[4,192,256]{2,1,0:T(8,128)(2,1)}), bf16[4,192,256]{2,1,0:T(8,128)(2,1)S(1)}, u32[]{:S(2)}, u32[]{:S(2)}) async-start(bf16[4,192,256]{2,1,0:T(8,128)(2,1)} %broadcast_in_dim.53), calls=%async_computation.6 | async-start | bytes 786432 | tf_op jit(solution)/shard_map/all_to_all | solution.py:43
where the time goes:
time: 169 us; the launch traced here: 168 us
  blocking collectives  50.1 us (30%)
  starting transfers between devices  43.8 us (26%)
  local copies, waits for them, and re-layouts  32.7 us (19%)
  waiting for transfers between devices  25.4 us (15%)
  other arithmetic  8.94 us (5%)
  matrix products  5.94 us (4%)
    all_to_all x2, blocking collectives, copies(): return lax.all_to_all(wide, axis, split_axis=0, concat_axis=0, tiled=True)  21.7 us
    all_to_all x2, blocking collectives, scatter_sum(): got = lax.all_to_all(low, axis, split_axis=0, concat_axis=0, tiled=True)  20.4 us
    ppermute x2, starting transfers between devices, padded_2(): lax.ppermute(head, axis, [((i + 1) % count, i) for i in range(count)])  17 us
    all_to_all x1, starting transfers between devices, on_device(): lax.all_to_all(mixed_grad, TM, split_axis=0, concat_axis=1, tiled=True)  10.3 us
    all_to_all x1, waiting for transfers between devices, on_device(): lax.all_to_all(mixed_grad, TM, split_axis=0, concat_axis=1, tiled=True)  9.85 us
    ppermute x2, waiting for transfers between devices, padded_2(): lax.ppermute(tail, axis, [(i, (i + 1) % count) for i in range(count)])  8.5 us
    all_gather x1, blocking collectives, sum_over_devices(): rows = lax.all_gather(rows, 'core', axis=0, tiled=True)  7.95 us
    another operation x9, local copies, waits for them, and re-layouts, on_device(): taps_part = jnp.stack(taps_rows, axis=0)  7.14 us
  transfers between devices with their start and end apart: 8, of which 6 were waited for; matrix products, arithmetic and copies ran while one was open for 12% of the time, Pallas kernels for 0%

commit v1 on v0

--- a/solution.py
+++ b/solution.py
@@ -100,7 +100,9 @@
     for source in range(frames):
         mixed_acc = mixed_acc + time_mix[source][:, None, :] * cot_f[source][None, :, :]
     mixed_grad = mixed_acc.astype(jnp.bfloat16)
-    back_grad = lax.all_to_all(mixed_grad, TM, split_axis=0, concat_axis=1, tiled=True)
+    pieces = jnp.split(mixed_grad, lax.axis_size(TM), axis=0)
+    received = lax.all_to_all(jnp.stack(pieces), TM, 0, 0)
+    back_grad = jnp.concatenate(received, axis=1)
     mixed_rows = back_grad.reshape(pixels, C)
     point_part = jnp.dot(spread_low.T, mixed_rows, preferred_element_type=jnp.float32)
     spread_grad = jnp.dot(mixed_rows, point_weight.T, preferred_element_type=jnp.float32).astype(

time: 169 us -> 169 us (level)
  no operation moved by 1% of the time
where the time goes in v1:
time: 169 us; the launch traced here: 168 us
  blocking collectives  50.1 us (30%)
  starting transfers between devices  43.8 us (26%)
  local copies, waits for them, and re-layouts  32.7 us (19%)
  waiting for transfers between devices  25.4 us (15%)
  other arithmetic  8.99 us (5%)
  matrix products  5.94 us (4%)
    all_to_all x2, blocking collectives, copies(): return lax.all_to_all(wide, axis, split_axis=0, concat_axis=0, tiled=True)  21.7 us
    all_to_all x2, blocking collectives, scatter_sum(): got = lax.all_to_all(low, axis, split_axis=0, concat_axis=0, tiled=True)  20.4 us
    ppermute x2, starting transfers between devices, padded_2(): lax.ppermute(head, axis, [((i + 1) % count, i) for i in range(count)])  17 us
    all_to_all x1, starting transfers between devices, on_device(): received = lax.all_to_all(jnp.stack(pieces), TM, 0, 0)  10.3 us
    all_to_all x1, waiting for transfers between devices, on_device(): received = lax.all_to_all(jnp.stack(pieces), TM, 0, 0)  9.85 us
    ppermute x2, waiting for transfers between devices, padded_2(): lax.ppermute(tail, axis, [(i, (i + 1) % count) for i in range(count)])  8.5 us
    all_gather x1, blocking collectives, sum_over_devices(): rows = lax.all_gather(rows, 'core', axis=0, tiled=True)  7.96 us
    another operation x9, local copies, waits for them, and re-layouts, on_device(): taps_part = jnp.stack(taps_rows, axis=0)  7.14 us
  transfers between devices with their start and end apart: 8, of which 6 were waited for; matrix products, arithmetic and copies ran while one was open for 12% of the time, Pallas kernels for 0%

profile of v1, /device:TPU:1, one launch (start us, length us, event | category | flops | bytes accessed | tf_op | source)
XLA Modules:
  0.0 167.9 jit_solution(15891443527590837143)
XLA Ops:
  1.4 1.0 convert_element_type.105
  3.5 10.3 %all-to-all-start = ((bf16[4,1,160,256]{3,2,1,0:T(8,128)(2,1)}), bf16[4,1,160,256]{3,2,1,0:T(8,128)(2,1)S(1)}, u32[]{:S(2)}, u32[]{:S(2)}) async-start(bf16[4,1,160,256]{3,2,1,0:T(8,128)(2,1)} %pad_maximum_fusion.2), calls=%async_computation | async-start | bytes 655360 | tf_op jit(solution)/shard_map/all_to_all | solution.py:104
  13.9 9.8 %all-to-all-done = bf16[4,1,160,256]{3,2,1,0:T(8,128)(2,1)S(1)} async-done(((bf16[4,1,160,256]{3,2,1,0:T(8,128)(2,1)}), bf16[4,1,160,256]{3,2,1,0:T(8,128)(2,1)S(1)}, u32[]{:S(2)}, u32[]{:S(2)}) %all-to-all-start) | async-done | bytes 327712 | tf_op jit(solution)/shard_map/all_to_all | solution.py:104
  26.6 11.4 %collective-permute-start.1 = (bf16[20,1,256]{2,0,1:T(8,128)(2,1)S(1)}, bf16[20,1,256]{2,0,1:T(8,128)(2,1)S(1)}, u32[]{:S(2)}, u32[]{:S(2)}) collective-permute-start(bf16[20,1,256]{2,0,1:T(8,128)(2,1)S(1)} %fusion.49), channel_id=1, source_target_pairs={{1,0},{2,1},{3,2},{4,3},{5,4},{6,5},{7,6},{8,7},{9,8},{10,9},{11,1... | collective-permute-start | bytes 30728 | tf_op jit(solution)/shard_map/ppermute | solution.py:26
  38.6 1.9 %collective-permute-start = (bf16[20,1,256]{2,0,1:T(8,128)(2,1)S(1)}, bf16[20,1,256]{2,0,1:T(8,128)(2,1)S(1)}, u32[]{:S(2)}, u32[]{:S(2)}) collective-permute-start(bf16[20,1,256]{2,0,1:T(8,128)(2,1)S(1)} %fusion.48), channel_id=1, source_target_pairs={{0,1},{1,2},{2,3},{3,4},{4,5},{5,6},{6,7},{7,8},{8,9},{9,10},{10,1... | collective-permute-start | bytes 30728 | tf_op jit(solution)/shard_map/ppermute | solution.py:24
  40.6 1.0 copy.116
  41.6 2.5 %reshape.140 = bf16[640,1024]{1,0:T(8,128)(2,1)S(1)} reshape(bf16[1,2560,256]{2,1,0:T(8,128)(2,1)} %param.16) | data formatting | bytes 2621440 | tf_op jit(solution)/shard_map/reshape | solution.py:70
  44.1 1.2 slice.277
  45.4 3.7 %collective-permute-done = bf16[20,1,256]{2,0,1:T(8,128)(2,1)S(1)} collective-permute-done((bf16[20,1,256]{2,0,1:T(8,128)(2,1)S(1)}, bf16[20,1,256]{2,0,1:T(8,128)(2,1)S(1)}, u32[]{:S(2)}, u32[]{:S(2)}) %collective-permute-start) | collective-permute-done | bytes 10272 | tf_op jit(solution)/shard_map/ppermute | solution.py:24
  50.9 5.7 %collective-permute-start.3 = (bf16[1,20,1,256]{3,1,2,0:T(8,128)(2,1)S(1)}, bf16[1,20,1,256]{3,1,2,0:T(8,128)(2,1)S(1)}, u32[]{:S(2)}, u32[]{:S(2)}) collective-permute-start(bf16[1,20,1,256]{3,1,2,0:T(8,128)(2,1)S(1)} %copy.134), channel_id=1, source_target_pairs={{1,0},{2,1},{3,2},{4,3},{5,4},{6,5},{7,6},{8,7},{9,8},{10,9},{11,1... | collective-permute-start | bytes 30728 | tf_op jit(solution)/shard_map/ppermute | solution.py:26
  56.6 1.9 %collective-permute-start.2 = (bf16[1,20,1,256]{3,1,2,0:T(8,128)(2,1)S(1)}, bf16[1,20,1,256]{3,1,2,0:T(8,128)(2,1)S(1)}, u32[]{:S(2)}, u32[]{:S(2)}) collective-permute-start(bf16[1,20,1,256]{3,1,2,0:T(8,128)(2,1)S(1)} %copy.133), channel_id=1, source_target_pairs={{0,1},{1,2},{2,3},{3,4},{4,5},{5,6},{6,7},{7,8},{8,9},{9,10},{10,1... | collective-permute-start | bytes 30728 | tf_op jit(solution)/shard_map/ppermute | solution.py:24
  58.5 1.6 convolution_bitcast_fusion
  62.3 4.8 %collective-permute-done.2 = bf16[1,20,1,256]{3,1,2,0:T(8,128)(2,1)S(1)} collective-permute-done((bf16[1,20,1,256]{3,1,2,0:T(8,128)(2,1)S(1)}, bf16[1,20,1,256]{3,1,2,0:T(8,128)(2,1)S(1)}, u32[]{:S(2)}, u32[]{:S(2)}) %collective-permute-start.2) | collective-permute-done | bytes 10272 | tf_op jit(solution)/shard_map/ppermute | solution.py:24
  70.0 3.4 %reduce.8 = bf16[640,256]{1,0:T(8,128)(2,1)} reduce(bf16[640,1,256]{2,1,0:T(2,128)(2,1)S(1)} %bitcast.117, bf16[]{:T(256)} %broadcast.133), dimensions={1}, to_apply=%bitcast.106.reduce_sub_computation | reduce | bytes 655362
  73.5 1.8 %reshape.196 = bf16[4,2,20480]{2,1,0:T(2,128)(2,1)} reshape(bf16[640,256]{1,0:T(8,128)(2,1)} %reduce.8) | data formatting | bytes 655360
  75.2 6.4 %all-to-all-start.1 = ((bf16[4,2,20480]{2,1,0:T(2,128)(2,1)}), bf16[4,2,20480]{2,1,0:T(2,128)(2,1)S(1)}, u32[]{:S(2)}, u32[]{:S(2)}) async-start(bf16[4,2,20480]{2,1,0:T(2,128)(2,1)} %reshape.196), calls=%async_computation.1 | async-start | bytes 655360 | tf_op jit(solution)/shard_map/all_to_all | solution.py:94
  88.7 1.0 fusion.53
  89.7 1.7 %all-to-all-done.1 = bf16[4,2,20480]{2,1,0:T(2,128)(2,1)S(1)} async-done(((bf16[4,2,20480]{2,1,0:T(2,128)(2,1)}), bf16[4,2,20480]{2,1,0:T(2,128)(2,1)S(1)}, u32[]{:S(2)}, u32[]{:S(2)}) %all-to-all-start.1) | async-done | bytes 327712 | tf_op jit(solution)/shard_map/all_to_all | solution.py:94
  91.8 1.1 copy.115
  92.8 1.6 convolution_bitcast_fusion.1
  96.1 3.0 %concatenate.24 = f32[1536,256]{0,1:T(8,128)S(1)} concatenate(f32[1024,256]{0,1:T(8,128)S(1)} %copy-done.1, f32[256,256]{0,1:T(8,128)S(1)} %copy-done.6, f32[16,256]{0,1:T(8,128)} %copy.119, f32[1,256]{0,1:T(8,128)} %copy.120, f32[1,256]{0,1:T(8,128)} %copy.121, f32[1,256]{0,1:T(8,128)} %copy.122, f32[1,256]{0,1:T(8,128)} %copy.123, f32[1,256]{0,1:T(8,128)} %copy.124, ...), dimensions={0} | concatenate | bytes 3145728 | tf_op jit(solution)/shard_map/concatenate | solution.py:146
  99.2 2.8 %collective-permute-start.4 = (bf16[768,256]{0,1:T(8,128)(2,1)S(1)}, bf16[768,256]{0,1:T(8,128)(2,1)S(1)}, u32[]{:S(2)}, u32[]{:S(2)}) collective-permute-start(bf16[768,256]{0,1:T(8,128)(2,1)S(1)} %dynamic-slice_convert_fusion), channel_id=1, source_target_pairs={{0,128},{128,0},{1,129},{129,1},{2,130},{130,2},{3,131},{131,3},{4... | collective-permute-start | bytes 1179656 | tf_op jit(solution)/shard_map/ppermute | solution.py:51
  102.0 1.3 collective-permute-done.4
  103.6 10.2 %all_to_all.42 = bf16[4,192,256]{2,1,0:T(8,128)(2,1)S(1)} all-to-all(bf16[4,192,256]{2,1,0:T(8,128)(2,1)S(1)} %bitcast.119), channel_id=1, replica_groups=mesh['yh'=2,'core'=2,'x'=4,'z'=8,'yl'=4] {'x'}, dimensions={0} | all-to-all | bytes 786432 | tf_op jit(solution)/shard_map/all_to_all | solution.py:36
  113.9 10.2 %all_to_all.43 = bf16[8,24,256]{2,1,0:T(8,128)(2,1)S(1)} all-to-all(bf16[8,24,256]{2,1,0:T(8,128)(2,1)S(1)} %bitcast.124), channel_id=1, replica_groups=mesh['yh'=2,'core'=2,'x'=4,'z'=8,'yl'=4] {'z'}, dimensions={0} | all-to-all | bytes 196608 | tf_op jit(solution)/shard_map/all_to_all | solution.py:36
  124.1 11.8 %all_to_all.44 = bf16[8,24,256]{2,1,0:T(8,128)(2,1)S(1)} all-to-all(bf16[8,24,256]{2,1,0:T(8,128)(2,1)S(1)} %broadcast_in_dim.50), channel_id=1, replica_groups=mesh['yh'=2,'core'=2,'x'=4,'z'=8,'yl'=4] {'yh','yl'}, dimensions={0} | all-to-all | bytes 196608 | tf_op jit(solution)/shard_map/all_to_all | solution.py:43
  135.9 10.0 %all_to_all.45 = bf16[8,24,256]{2,1,0:T(8,128)(2,1)S(1)} all-to-all(bf16[8,24,256]{2,1,0:T(8,128)(2,1)S(1)} %broadcast_in_dim.51), channel_id=1, replica_groups=mesh['yh'=2,'core'=2,'x'=4,'z'=8,'yl'=4] {'z'}, dimensions={0} | all-to-all | bytes 196608 | tf_op jit(solution)/shard_map/all_to_all | solution.py:43
  146.6 3.5 %all-to-all-start.6 = ((bf16[4,192,256]{2,1,0:T(8,128)(2,1)}), bf16[4,192,256]{2,1,0:T(8,128)(2,1)S(1)}, u32[]{:S(2)}, u32[]{:S(2)}) async-start(bf16[4,192,256]{2,1,0:T(8,128)(2,1)} %broadcast_in_dim.53), calls=%async_computation.6 | async-start | bytes 786432 | tf_op jit(solution)/shard_map/all_to_all | solution.py:43
  150.7 1.6 reshape.141
  152.3 4.0 %all-to-all-done.6 = bf16[4,192,256]{2,1,0:T(8,128)(2,1)S(1)} async-done(((bf16[4,192,256]{2,1,0:T(8,128)(2,1)}), bf16[4,192,256]{2,1,0:T(8,128)(2,1)S(1)}, u32[]{:S(2)}, u32[]{:S(2)}) %all-to-all-start.6) | async-done | bytes 393248 | tf_op jit(solution)/shard_map/all_to_all | solution.py:43
  156.3 8.0 %all_gather.3 = bf16[1536,256]{1,0:T(8,128)(2,1)S(1)} all-gather(bf16[768,256]{1,0:T(8,128)(2,1)S(1)} %bitcast.120), channel_id=1, replica_groups=mesh['yh'=2,'core'=2,'x'=4,'z'=8,'yl'=4] {'core'}, dimensions={0}, use_global_device_ids=true | all-gather | bytes 1179648 | tf_op jit(solution)/shard_map/all_gather | solution.py:59
  166.3 1.0 slice.290
  (93 shorter events, 25.8 us)
Async XLA Ops:
  0.6 49.4 %copy-start = (bf16[1024,256]{1,0:T(8,128)(2,1)S(1)}, bf16[1024,256]{1,0:T(8,128)(2,1)}, u32[]{:S(2)}) copy-start(bf16[1024,256]{1,0:T(8,128)(2,1)} %param.17) | copy-start | bytes 1572868
  2.5 11.3 %copy-start.10 = (s32[1,2,20]{2,1,0:T(2,128)S(1)}, s32[1,2,20]{2,1,0:T(2,128)}, u32[]{:S(2)}) copy-start(s32[1,2,20]{2,1,0:T(2,128)} %param.22) | copy-start | bytes 484
  2.5 11.3 %copy-start.9 = (f32[9,256]{1,0:T(8,128)S(1)}, f32[9,256]{1,0:T(8,128)}, u32[]{:S(2)}) copy-start(f32[9,256]{1,0:T(8,128)} %param.19) | copy-start | bytes 27652
  2.5 21.2 %copy-start.7 = (bf16[256,256]{1,0:T(8,128)(2,1)S(1)}, bf16[256,256]{1,0:T(8,128)(2,1)}, u32[]{:S(2)}) copy-start(bf16[256,256]{1,0:T(8,128)(2,1)} %param.20) | copy-start | bytes 393220
  3.5 20.2 %all-to-all-start = ((bf16[4,1,160,256]{3,2,1,0:T(8,128)(2,1)}), bf16[4,1,160,256]{3,2,1,0:T(8,128)(2,1)S(1)}, u32[]{:S(2)}, u32[]{:S(2)}) async-start(bf16[4,1,160,256]{3,2,1,0:T(8,128)(2,1)} %pad_maximum_fusion.2), calls=%async_computation | async-start | bytes 655360 | tf_op jit(solution)/shard_map/all_to_all | solution.py:104
  24.4 16.1 %copy-start.3 = (bf16[4,160,256]{2,1,0:T(8,128)(2,1)S(1)}, bf16[4,160,256]{2,1,0:T(8,128)(2,1)}, u32[]{:S(2)}) copy-start(bf16[4,160,256]{2,1,0:T(8,128)(2,1)} %param.23) | copy-start | bytes 983044
  25.0 0.9 copy-start.2
  26.6 18.8 %collective-permute-start.1 = (bf16[20,1,256]{2,0,1:T(8,128)(2,1)S(1)}, bf16[20,1,256]{2,0,1:T(8,128)(2,1)S(1)}, u32[]{:S(2)}, u32[]{:S(2)}) collective-permute-start(bf16[20,1,256]{2,0,1:T(8,128)(2,1)S(1)} %fusion.49), channel_id=1, source_target_pairs={{1,0},{2,1},{3,2},{4,3},{5,4},{6,5},{7,6},{8,7},{9,8},{10,9},{11,1... | collective-permute-start | bytes 30728 | tf_op jit(solution)/shard_map/ppermute | solution.py:26
  38.6 10.4 %collective-permute-start = (bf16[20,1,256]{2,0,1:T(8,128)(2,1)S(1)}, bf16[20,1,256]{2,0,1:T(8,128)(2,1)S(1)}, u32[]{:S(2)}, u32[]{:S(2)}) collective-permute-start(bf16[20,1,256]{2,0,1:T(8,128)(2,1)S(1)} %fusion.48), channel_id=1, source_target_pairs={{0,1},{1,2},{2,3},{3,4},{4,5},{5,6},{6,7},{7,8},{8,9},{9,10},{10,1... | collective-permute-start | bytes 30728 | tf_op jit(solution)/shard_map/ppermute | solution.py:24
  44.1 5.9 %copy-start.11 = (f32[256]{0:T(256)S(1)}, f32[256]{0:T(256)}, u32[]{:S(2)}) copy-start(f32[256]{0:T(256)} %param.18) | copy-start | bytes 3076
  50.8 9.3 %copy-start.4 = (bf16[640,256]{1,0:T(8,128)(2,1)}, bf16[640,256]{1,0:T(8,128)(2,1)S(1)}, u32[]{:S(2)}) copy-start(bf16[640,256]{1,0:T(8,128)(2,1)S(1)} %get-tuple-element.53) | copy-start | bytes 983044
  50.9 10.8 %collective-permute-start.3 = (bf16[1,20,1,256]{3,1,2,0:T(8,128)(2,1)S(1)}, bf16[1,20,1,256]{3,1,2,0:T(8,128)(2,1)S(1)}, u32[]{:S(2)}, u32[]{:S(2)}) collective-permute-start(bf16[1,20,1,256]{3,1,2,0:T(8,128)(2,1)S(1)} %copy.134), channel_id=1, source_target_pairs={{1,0},{2,1},{3,2},{4,3},{5,4},{6,5},{7,6},{8,7},{9,8},{10,9},{11,1... | collective-permute-start | bytes 30728 | tf_op jit(solution)/shard_map/ppermute | solution.py:26
  56.6 10.5 %collective-permute-start.2 = (bf16[1,20,1,256]{3,1,2,0:T(8,128)(2,1)S(1)}, bf16[1,20,1,256]{3,1,2,0:T(8,128)(2,1)S(1)}, u32[]{:S(2)}, u32[]{:S(2)}) collective-permute-start(bf16[1,20,1,256]{3,1,2,0:T(8,128)(2,1)S(1)} %copy.133), channel_id=1, source_target_pairs={{0,1},{1,2},{2,3},{3,4},{4,5},{5,6},{6,7},{7,8},{8,9},{9,10},{10,1... | collective-permute-start | bytes 30728 | tf_op jit(solution)/shard_map/ppermute | solution.py:24
  75.2 16.2 %all-to-all-start.1 = ((bf16[4,2,20480]{2,1,0:T(2,128)(2,1)}), bf16[4,2,20480]{2,1,0:T(2,128)(2,1)S(1)}, u32[]{:S(2)}, u32[]{:S(2)}) async-start(bf16[4,2,20480]{2,1,0:T(2,128)(2,1)} %reshape.196), calls=%async_computation.1 | async-start | bytes 655360 | tf_op jit(solution)/shard_map/all_to_all | solution.py:94
  89.7 3.1 %copy-start.8 = (bf16[4,160,256]{1,0,2:T(4,128)(2,1)S(1)}, bf16[4,160,256]{1,0,2:T(4,128)(2,1)}, u32[]{:S(2)}) copy-start(bf16[4,160,256]{1,0,2:T(4,128)(2,1)} %copy.116) | copy-start | bytes 983044
  92.8 3.3 %copy-start.1 = (f32[1024,256]{0,1:T(8,128)S(1)}, f32[1024,256]{0,1:T(8,128)}, u32[]{:S(2)}) copy-start(f32[1024,256]{0,1:T(8,128)} %convolution_bitcast_fusion) | copy-start | bytes 3145732
  92.8 3.3 %copy-start.6 = (f32[256,256]{0,1:T(8,128)S(1)}, f32[256,256]{0,1:T(8,128)}, u32[]{:S(2)}) copy-start(f32[256,256]{0,1:T(8,128)} %fusion.53) | copy-start | bytes 786436
  99.2 4.1 %collective-permute-start.4 = (bf16[768,256]{0,1:T(8,128)(2,1)S(1)}, bf16[768,256]{0,1:T(8,128)(2,1)S(1)}, u32[]{:S(2)}, u32[]{:S(2)}) collective-permute-start(bf16[768,256]{0,1:T(8,128)(2,1)S(1)} %dynamic-slice_convert_fusion), channel_id=1, source_target_pairs={{0,128},{128,0},{1,129},{129,1},{2,130},{130,2},{3,131},{131,3},{4... | collective-permute-start | bytes 1179656 | tf_op jit(solution)/shard_map/ppermute | solution.py:51
  113.8 36.3 %copy-start.5 = (bf16[640,256]{1,0:T(8,128)(2,1)S(1)}, bf16[640,256]{1,0:T(8,128)(2,1)}, u32[]{:S(2)}) copy-start(bf16[640,256]{1,0:T(8,128)(2,1)} %copy-done.4) | copy-start | bytes 983044
  146.6 9.7 %all-to-all-start.6 = ((bf16[4,192,256]{2,1,0:T(8,128)(2,1)}), bf16[4,192,256]{2,1,0:T(8,128)(2,1)S(1)}, u32[]{:S(2)}, u32[]{:S(2)}) async-start(bf16[4,192,256]{2,1,0:T(8,128)(2,1)} %broadcast_in_dim.53), calls=%async_computation.6 | async-start | bytes 786432 | tf_op jit(solution)/shard_map/all_to_all | solution.py:43
